TPU v7x, 32 devices: a whole 2x2x4 slice. The times are simulated.
32 devices in a mesh: grp: 2 (over y), rcv: 16 (over z, x, core).
Axes of the slice: x: 2, y: 2, z: 4, core: 2. Of those that a mesh axis runs over, the one named last changes fastest.
Arguments:
- traces: bfloat16 [2, 3072, 5376], P(None, ('grp', 'rcv')), parts along dimension 1, may hold values from -17 to 17, as said below
- sketch: bfloat16 [2, 96, 5376], P(None, None, 'rcv'), may hold values from -0.0625 to 0.0625
Outputs:
- basis: float32 [2, 3072, 96], P(None, ('grp', 'rcv')), parts along dimension 1
- coeffs: float32 [2, 192, 5376], P(None, 'grp', 'rcv'), parts along dimension 1
There are 2 independent parts, one for each index of `grp`. A program takes and returns all parts, laid end to end along the dimension named above; an argument that names none is the same for every part. Nothing has to cross between parts.
Inputs may be any that keep to these rules, and one draw needn't show every extreme that they name: `traces`: complex data, real part at index 0 and imaginary part at index 1 of the first dimension.
All inputs are finite; a program needn't handle non-finite values.
Results may differ from a plain program's by a relative error of at most 0.0015.
Values may be sent and summed in bfloat16 or wider, within the bound.
A program may use at most 64 MiB of HBM per device.

v0:
```python
import math

import jax
import jax.numpy as jnp
from jax import lax
from jax.sharding import PartitionSpec as P


def precise_dot(left, right):
    return jnp.dot(left, right, precision=lax.Precision.HIGHEST, preferred_element_type=jnp.float32)


def complex_product(left, right):
    return (
        precise_dot(left[0], right[0]) - precise_dot(left[1], right[1]),
        precise_dot(left[0], right[1]) + precise_dot(left[1], right[0]),
    )


def inner_rows(left, right):
    return lax.dot_general(
        left,
        right,
        (((0,), (0,)), ((), ())),
        precision=lax.Precision.HIGHEST,
        preferred_element_type=jnp.float32,
    )


def coarse_rows(left, right):
    return lax.dot_general(
        left, right, (((0,), (0,)), ((), ())), preferred_element_type=jnp.float32
    )


def across_sources(left, right):
    return lax.dot_general(
        left, right, (((1,), (1,)), ((), ())), preferred_element_type=jnp.float32
    )


def factor(gram):
    count = gram[0].shape[0]
    embed = jnp.stack(
        [jnp.stack([gram[0], -gram[1]], axis=-1), jnp.stack([gram[1], gram[0]], axis=-1)], axis=1
    )
    embed = embed.reshape(2 * count, 2 * count)
    lower = jnp.linalg.cholesky(embed)
    ident = jnp.eye(2 * count, dtype=jnp.float32)
    lower_inv = jax.scipy.linalg.solve_triangular(lower, ident, lower=True)
    low_re = lower[0::2, 0::2]
    low_im = lower[1::2, 0::2]
    linv_re = lower_inv[0::2, 0::2]
    linv_im = lower_inv[1::2, 0::2]
    return (low_re.T, -low_im.T, linv_re.T, -linv_im.T)


def per_device(traces, sketch):
    rows = traces.shape[1]
    width = sketch.shape[1]
    piece = lax.all_gather(sketch, "rcv", axis=2, tiled=True)
    columns = traces
    sum_re = across_sources(columns[0], piece[0]) - across_sources(columns[1], piece[1])
    sum_im = across_sources(columns[0], piece[1]) + across_sources(columns[1], piece[0])
    gram_re = inner_rows(sum_re, sum_re) + inner_rows(sum_im, sum_im)
    gram_im = inner_rows(sum_re, sum_im) - inner_rows(sum_im, sum_re)
    total_re, total_im = lax.psum((gram_re, gram_im), "rcv")
    factors = factor((total_re, total_im))
    ortho_re, ortho_im = complex_product((sum_re, sum_im), (factors[2], factors[3]))
    scale = math.sqrt(rows * lax.axis_size("rcv"))
    basis = jnp.stack([ortho_re * scale, ortho_im * scale])
    rounded_re = ortho_re.astype(jnp.bfloat16)
    rounded_im = ortho_im.astype(jnp.bfloat16)
    share = traces.shape[2] // lax.axis_size("rcv")
    columns = traces
    block_re = coarse_rows(columns[0], rounded_re) + coarse_rows(columns[1], rounded_im)
    block_im = coarse_rows(columns[1], rounded_re) - coarse_rows(columns[0], rounded_im)
    summed = lax.psum_scatter(
        jnp.concatenate([block_re, block_im], axis=1), "rcv", scatter_dimension=0, tiled=True
    )
    coeffs = jnp.transpose(summed.reshape(share, 2, width), (1, 2, 0))
    return (basis, coeffs)


def solution(mesh):
    return jax.shard_map(
        per_device,
        mesh=mesh,
        in_specs=(P(None, ("grp", "rcv"), None), P(None, None, "rcv")),
        out_specs=(P(None, ("grp", "rcv"), None), P(None, "grp", "rcv")),
        check_vma=False,
    )
```

profile of v0, /device:TPU:0, one launch (start us, length us, event | category | flops | bytes accessed | tf_op | source)
XLA Modules:
  0.0 338.2 jit_solution(4600300290485290631)
XLA Ops:
  7.2 1.7 copy.14
  9.1 47.9 %all-gather.2.cloned.1.call-done = bf16[2,96,5376]{1,0,2:T(2,128)(2,1)} async-done(((bf16[2,96,336]{1,0,2:T(2,128)(2,1)}), bf16[2,96,5376]{1,0,2:T(2,128)(2,1)}) %all-gather.2.cloned.1.call-update) | async-done | bytes 2064400 | tf_op jit(solution)/shard_map/all_gather | solution.py:61
  56.9 8.1 %fusion.43 = (bf16[1,96,5376]{1,0,2:T(2,128)(2,1)}, bf16[1,96,5376]{1,0,2:T(2,128)(2,1)S(1)}) fusion(bf16[2,96,5376]{1,0,2:T(2,128)(2,1)} %all-gather.2.cloned.1.call-done), kind=kLoop, calls=%fused_computation.84 | loop fusion | bytes 4128768 | tf_op jit(solution)/shard_map/slice | solution.py:63
  65.0 6.5 %copy.24 = bf16[1,96,5376]{2,1,0:T(8,128)(2,1)} copy(bf16[1,96,5376]{1,0,2:T(2,128)(2,1)} %get-tuple-element.24) | data formatting | bytes 2064384
  71.5 4.7 %copy.23 = bf16[1,96,5376]{2,1,0:T(8,128)(2,1)} copy(bf16[1,96,5376]{1,0,2:T(2,128)(2,1)S(1)} %get-tuple-element.25) | data formatting | bytes 2064384
  76.2 2.1 fusion.3
  78.3 0.1 copy-done
  78.4 1.7 fusion.12
  80.1 0.4 convolution_add_fusion.3
  80.6 0.4 convolution_subtract_fusion.4
  81.0 0.3 fusion.44
  81.3 0.3 fusion.45
  81.5 0.9 convolution_subtract_fusion.3
  82.4 0.9 fusion.2
  83.3 0.2 reduce-scatter.4.cloned.1.call-start
  83.6 87.7 %all-reduce.6.cloned.1.call-done = (f32[96,96,1]{1,0,2:T(8,128)}, f32[96,96]{1,0:T(8,128)}) async-done(((f32[96,96,1]{1,0,2:T(8,128)}, f32[96,96]{1,0:T(8,128)}), (f32[96,96,1]{1,0,2:T(8,128)}, f32[96,96]{1,0:T(8,128)})) %all-reduce.6.cloned.1.call-update) | async-done | bytes 73744 | tf_op jit(solution)/shard_map/psum | solution.py:67
  171.3 0.8 negate_bitcast_fusion
  172.1 0.9 maximum_bitcast_fusion
  173.0 5.1 %copy.17 = f32[96,2,96,2]{3,2,1,0:T(8,128)} copy(f32[96,2,96,2]{2,0,3,1:T(8,128)S(1)} %pad_maximum_fusion.1) | data formatting | bytes 294912 | tf_op jit(solution)/shard_map/stack | solution.py:44
  178.1 7.7 %reshape.33 = f32[192,192]{1,0:T(8,128)S(1)} reshape(f32[96,2,96,2]{3,2,1,0:T(8,128)} %copy.17) | data formatting | bytes 294912 | tf_op jit(solution)/shard_map/reshape | solution.py:47
  185.8 0.1 copy.18
  186.0 11.7 %cholesky.51 = f32[128,128]{1,0:T(8,128)S(1)} custom-call(f32[128,128]{1,0:T(8,128)S(1)} %cholesky.124), custom_call_target="Cholesky" | custom-call | tf_op jit(solution)/shard_map/jit(cholesky)/cholesky | solution.py:48
  197.8 9.8 %custom-call.15 = f32[1,128,128]{1,2,0:T(8,128)S(1)} custom-call(f32[1,128,128]{2,1,0:T(8,128)S(1)} %get-tuple-element.27), custom_call_target="InvertDiagBlocksLowerTriangular" | custom-call | tf_op jit(solution)/shard_map/jit(cholesky)/cholesky | solution.py:48
  207.6 0.2 constant_dynamic-update-slice_fusion.1
  207.8 0.2 convolution_subtract_fusion.5
  208.0 5.8 %cholesky.110 = f32[64,64]{1,0:T(8,128)S(1)} custom-call(f32[64,64]{1,0:T(8,128)S(1)} %convolution_subtract_fusion.5), custom_call_target="Cholesky" | custom-call | tf_op jit(solution)/shard_map/jit(cholesky)/cholesky | solution.py:48
  213.8 0.6 compare_reduce_fusion
  214.5 0.6 compare_reduce_fusion.1
  216.5 0.1 fusion.30
  216.6 19.9 %custom-call.16 = f32[2,128,128]{1,2,0:T(8,128)S(1)} custom-call(f32[2,128,128]{2,1,0:T(8,128)S(1)} %pad_maximum_fusion.3), custom_call_target="InvertDiagBlocksLowerTriangular" | custom-call | tf_op jit(solution)/shard_map/jit(_solve_triangular)/triangular_solve | solution.py:50
  236.5 0.3 fusion.28
  236.8 0.3 convolution_subtract_fusion.1
  237.1 0.3 fusion.37
  237.4 1.3 slice.81
  238.7 1.3 slice.82
  240.0 0.2 fusion.46
  240.2 0.2 fusion.33
  240.4 0.2 convolution_subtract_fusion.2
  240.6 0.5 fusion.15
  241.1 0.5 fusion.6
  241.5 0.2 convolution_add_fusion.1
  241.7 0.5 fusion
  242.2 0.5 fusion.1
  242.7 2.3 pad_maximum_fusion
  245.0 5.7 %copy.21 = f32[5376,192]{1,0:T(8,128)} copy(f32[5376,192]{0,1:T(8,128)} %pad_maximum_fusion) | data formatting | bytes 8257536
  250.8 0.7 pad_maximum_fusion.4
  251.4 78.4 %reduce-scatter.4.cloned.1.call-done = f32[336,192]{1,0:T(8,128)} async-done(((f32[5376,192]{1,0:T(8,128)}), f32[336,192]{1,0:T(8,128)}) %reduce-scatter.4.cloned.1.call-update) | async-done | bytes 258064
  329.8 1.8 copy.22
  (25 shorter events, 0.4 us)
Async XLA Ops:
  7.2 49.8 %all-gather.2.cloned.1.call-start = ((), (), s32[]{:S(2)}) async-start(), calls=%async_computation.1 | async-start | bytes 2924544 | tf_op jit(solution)/shard_map/all_gather | solution.py:61
  9.0 162.3 %all-reduce.6.cloned.1.call-start = ((), (), s32[]{:S(2)}) async-start(), calls=%async_computation.3 | async-start | bytes 196608 | tf_op jit(solution)/shard_map/psum | solution.py:67
  76.2 2.2 copy-start
  76.2 3.9 %copy-start.2 = (bf16[1,96,5376]{2,1,0:T(8,128)(2,1)S(1)}, bf16[1,96,5376]{2,1,0:T(8,128)(2,1)}, u32[]{:S(2)}) copy-start(bf16[1,96,5376]{2,1,0:T(8,128)(2,1)} %copy.23) | copy-start | bytes 3096580
  78.4 2.2 copy-start.1
  83.3 246.5 %reduce-scatter.4.cloned.1.call-start = ((), (), s32[]{:S(2)}) async-start(), calls=%async_computation.2 | async-start | bytes 5849088
Sparse Core Ops, SparseCore 0:
  10.8 46.0 all-gather.1
  83.4 87.7 all-reduce.5
  250.8 78.8 reduce-scatter.3
where the time goes:
time: 339 us; the launch traced here: 338 us
  waiting for transfers between devices  214 us (63%)
  other arithmetic  53.5 us (16%)
  local copies, waits for them, and re-layouts  44.2 us (13%)
  between operations  15.3 us (5%)
  matrix products  10.8 us (3%)
    psum x1, waiting for transfers between devices, per_device(): total_re, total_im = lax.psum((gram_re, gram_im), 'rcv')  87.7 us
    unnamed x4, waiting for transfers between devices  78.4 us
    all_gather x1, waiting for transfers between devices, per_device(): piece = lax.all_gather(sketch, 'rcv', axis=2, tiled=True)  47.9 us
    another operation x7, other arithmetic, factor(): lower = jnp.linalg.cholesky(embed)  28.7 us
    unnamed x11, local copies, waits for them, and re-layouts  20.6 us
    another operation x7, other arithmetic, factor(): lower_inv = jax.scipy.linalg.solve_triangular(lower, ident, lower=True)  20 us
    slice x1, local copies, waits for them, and re-layouts, per_device(): piece[1]  8.06 us
    reshape x2, local copies, waits for them, and re-layouts, factor(): embed = embed.reshape(2 * count, 2 * count)  7.84 us
  transfers between devices with their start and end apart: 3, of which 3 were waited for; matrix products, arithmetic and copies ran while one was open for 0% of the time, Pallas kernels for 0%

commit v1 on v0

v1 whole, which is shorter than its diff:
```python
import functools
import math

import jax
import jax.numpy as jnp
from jax import lax
from jax.experimental import pallas as pl
from jax.experimental.pallas import tpu as pltpu
from jax.sharding import PartitionSpec as P

VMEM = pltpu.VMEM
F32 = jnp.float32
BF16 = jnp.bfloat16
LIMIT = 67_000_000


def plan(n):
    chips = n // 2
    fast = max(d for d in range(1, chips + 1) if chips % d == 0 and d * d <= chips)
    return chips // fast, fast


def exact(left, right, dims):
    return lax.dot_general(
        left, right, (dims, ((), ())), precision=lax.Precision.HIGHEST, preferred_element_type=F32
    )


def remote(src, dst, send, recv, target):
    return pltpu.make_async_remote_copy(
        src_ref=src, dst_ref=dst, send_sem=send, recv_sem=recv,
        device_id={"rcv": target}, device_id_type=pl.DeviceIdType.MESH,
    )


def place(fast):
    me = lax.axis_index("rcv")
    chip = me // 2
    return me, chip // fast, chip % fast, me % 2


def greet(targets):
    barrier = pltpu.get_barrier_semaphore()
    for target in targets:
        pl.semaphore_signal(
            barrier, inc=1, device_id={"rcv": target}, device_id_type=pl.DeviceIdType.MESH
        )
    pl.semaphore_wait(barrier, len(targets))


def sketch_kernel(
    n, data, mine, sketched, gram_out,
    held, acc, own, pair_in, pair_sum, quick_in, line_in,
    up_send, down_send, side_send, core_send, recv,
    g_send, g_recv,
):
    slow, fast = plan(n)
    me, s, f, c = place(fast)
    half = sketched.shape[1]

    def index(a, b, e):
        return (a * fast + b) * 2 + e

    partner = index(s, f, 1 - c)
    sides = [index(s, (f + d) % fast, c) for d in range(1, fast)]
    lines = [index((s + d) % slow, f, c) for d in range(1, slow)]
    greet([partner] + sides + lines)

    def block(slot, first):
        return mine if first else held.at[slot]

    def to_up(slot, first=False):
        return remote(block(slot, first), held.at[slot], up_send.at[slot], recv.at[slot], index(jnp.minimum(s + 1, slow - 1), f, c))

    def to_down(slot, first=False):
        return remote(block(slot, first), held.at[slot], down_send.at[slot], recv.at[slot], index(jnp.maximum(s - 1, 0), f, c))

    def to_side(d, slot, first=False):
        return remote(block(slot, first), held.at[slot], side_send.at[d, slot], recv.at[slot], sides[d])

    def to_core(slot, first=False):
        return remote(block(slot, first), held.at[slot], core_send.at[slot], recv.at[slot], partner)

    def arrived(slot):
        remote(held.at[slot], held.at[slot], core_send.at[slot], recv.at[slot], partner).wait_recv()

    def add(slot, first=False):
        value = mine[...] if first else held[slot]
        acc[...] += lax.dot_general(
            data[slot], value, (((1,), (1,)), ((), ())), preferred_element_type=F32
        )

    pl.when(s < slow - 1)(lambda: to_up(me, True).start())
    pl.when(s > 0)(lambda: to_down(me, True).start())
    for d in range(fast - 1):
        to_side(d, me, True).start()
    to_core(me, True).start()
    acc[...] = jnp.zeros_like(acc)
    add(me, True)

    for d in range(1, slow):

        @pl.when(s - d >= 0)
        def _(d=d):
            slot = index(s - d, f, c)
            arrived(slot)
            pl.when(s < slow - 1)(lambda: to_up(slot).start())
            for e in range(fast - 1):
                to_side(e, slot).start()
            to_core(slot).start()
            add(slot)

        @pl.when(s + d < slow)
        def _(d=d):
            slot = index(s + d, f, c)
            arrived(slot)
            pl.when(s > 0)(lambda: to_down(slot).start())
            for e in range(fast - 1):
                to_side(e, slot).start()
            to_core(slot).start()
            add(slot)

    def across(b):
        for d in range(slow):
            for sign in ((1,) if d == 0 else (-1, 1)):

                @pl.when((s + sign * d >= 0) & (s + sign * d < slow))
                def _(d=d, sign=sign):
                    slot = index(s + sign * d, b, c)
                    arrived(slot)
                    to_core(slot).start()
                    add(slot)

    for d in range(1, fast):
        across((f + d) % fast)

    def other(b):
        for d in range(slow):
            for sign in ((1,) if d == 0 else (-1, 1)):

                @pl.when((s + sign * d >= 0) & (s + sign * d < slow))
                def _(d=d, sign=sign):
                    slot = index(s + sign * d, b, 1 - c)
                    arrived(slot)
                    add(slot)

    for d in range(fast):
        other((f + d) % fast)

    to_core(me, True).wait_send()
    pl.when(s < slow - 1)(lambda: to_up(me, True).wait_send())
    pl.when(s > 0)(lambda: to_down(me, True).wait_send())
    for e in range(fast - 1):
        to_side(e, me, True).wait_send()
    for d in range(1, slow):

        @pl.when(s - d >= 0)
        def _(d=d):
            slot = index(s - d, f, c)
            pl.when(s < slow - 1)(lambda: to_up(slot).wait_send())
            for e in range(fast - 1):
                to_side(e, slot).wait_send()
            to_core(slot).wait_send()

        @pl.when(s + d < slow)
        def _(d=d):
            slot = index(s + d, f, c)
            pl.when(s > 0)(lambda: to_down(slot).wait_send())
            for e in range(fast - 1):
                to_side(e, slot).wait_send()
            to_core(slot).wait_send()

    for d in range(1, fast):
        for a in range(slow):
            to_core(index(a, (f + d) % fast, c)).wait_send()

    rows = half
    width = sketched.shape[2]
    re = acc[:rows, :width] - acc[rows:, width:]
    im = acc[:rows, width:] + acc[rows:, :width]
    sketched[0] = re
    sketched[1] = im
    first = ((0,), (0,))
    gram_re = exact(re, re, first) + exact(im, im, first)
    gram_im = exact(re, im, first) - exact(im, re, first)
    row = lax.broadcasted_iota(jnp.int32, gram_re.shape, 0)
    col = lax.broadcasted_iota(jnp.int32, gram_re.shape, 1)
    own[...] = jnp.where(col >= row, gram_re, gram_im)

    step = remote(own, pair_in, g_send.at[0], g_recv.at[0], partner)
    step.start()
    step.wait()
    pair_sum[...] = own[...] + pair_in[...]
    steps = [
        remote(pair_sum, quick_in.at[d], g_send.at[1 + d], g_recv.at[1 + d], sides[d])
        for d in range(fast - 1)
    ]
    for step in steps:
        step.start()
    for step in steps:
        step.wait()
    total = pair_sum[...]
    for d in range(fast - 1):
        total = total + quick_in[d]
    line_in[s] = total
    steps = [
        remote(line_in.at[s], line_in.at[s], g_send.at[fast + d], g_recv.at[fast + d], lines[d])
        for d in range(slow - 1)
    ]
    for step in steps:
        step.start()
    for d in range(slow - 1):
        steps[d].wait()
    total = line_in[0]
    for a in range(1, slow):
        total = total + line_in[a]
    gram_out[...] = total


def factor_kernel(scale, gram, sketched, basis, weights):
    packed = gram[...]
    width = packed.shape[0]
    turned = packed.T
    row = lax.broadcasted_iota(jnp.int32, packed.shape, 0)
    col = lax.broadcasted_iota(jnp.int32, packed.shape, 1)
    g_re = jnp.where(col >= row, packed, turned)
    g_im = jnp.where(row > col, packed, jnp.where(row < col, -turned, 0.0))
    tile = 8
    count = width // tile
    re = [g_re[tile * i : tile * (i + 1)] for i in range(count)]
    im = [g_im[tile * i : tile * (i + 1)] for i in range(count)]
    lane = lax.broadcasted_iota(jnp.int32, (tile, width), 1)
    sub = lax.broadcasted_iota(jnp.int32, (tile, width), 0)
    for k in range(width):
        at, inside = divmod(k, tile)
        d = re[at][inside : inside + 1, k : k + 1]
        here = lane[:1] == k
        p_re = jnp.where(here, 1.0, re[at][inside : inside + 1, :])
        p_im = jnp.where(here, 0.0, im[at][inside : inside + 1, :])
        inv = 1.0 / d
        q_re = p_re * inv
        q_im = p_im * inv
        for i in range(at, count):
            c_re = re[i][:, k : k + 1]
            c_im = im[i][:, k : k + 1]
            old_re = jnp.where(lane == k, 0.0, re[i])
            old_im = jnp.where(lane == k, 0.0, im[i])
            new_re = old_re - (c_re * q_re - c_im * q_im)
            new_im = old_im - (c_re * q_im + c_im * q_re)
            if i == at:
                root = lax.rsqrt(d)
                new_re = jnp.where(sub > inside, new_re, jnp.where(sub == inside, jnp.where(lane > k, 0.0, p_re * root), re[i]))
                new_im = jnp.where(sub > inside, new_im, jnp.where(sub == inside, jnp.where(lane > k, 0.0, p_im * root), im[i]))
            re[i] = new_re
            im[i] = new_im
    l_re = jnp.concatenate(re, axis=0)
    l_im = jnp.concatenate(im, axis=0)
    s_re, s_im = sketched[0], sketched[1]
    last = ((1,), (1,))
    o_re = exact(s_re, l_re, last) + exact(s_im, l_im, last)
    o_im = exact(s_im, l_re, last) - exact(s_re, l_im, last)
    basis[0] = o_re * scale
    basis[1] = o_im * scale
    t_re, t_im = o_re.T, o_im.T
    rows = o_re.shape[0]
    weights[:width, :rows] = t_re.astype(BF16)
    weights[:width, rows:] = t_im.astype(BF16)
    weights[width:, :rows] = (-t_im).astype(BF16)
    weights[width:, rows:] = t_re.astype(BF16)


def project_kernel(
    n, data, weights, out,
    kept, away, from_core, side_out, side_in, line_out, line_in,
    c_send, c_recv, s_send, s_recv, u_send, u_recv, d_send, d_recv,
):
    slow, fast = plan(n)
    me, s, f, c = place(fast)

    def index(a, b, e):
        return (a * fast + b) * 2 + e

    partner = index(s, f, 1 - c)
    sides = [index(s, (f + d) % fast, c) for d in range(1, fast)]
    lines = [index((s + d) % slow, f, c) for d in range(1, slow)]
    greet([partner] + sides + lines)

    def product(slot):
        return jnp.dot(weights[...], data[slot], preferred_element_type=F32)

    def core_copy(t, d):
        return remote(away.at[d, t], from_core.at[d, t], c_send.at[d, t], c_recv.at[d, t], partner)

    def side_copy(t, d):
        return remote(side_out.at[d, t], side_in.at[d, t], s_send.at[d, t], s_recv.at[d, t], sides[d - 1])

    low = s < slow - s - 1

    def target(t):
        return jnp.where(low, slow - 1 - t, t)

    def begin(t, d):
        a, b = target(t), (f + d) % fast
        away[d, t] = product(index(a, b, 1 - c))
        core_copy(t, d).start()
        kept[d, t] = product(index(a, b, c))

    def middle(t, d):
        core_copy(t, d).wait()
        value = kept[d, t] + from_core[d, t]
        if d == 0:
            kept[0, t] = value
        else:
            side_out[d, t] = value.astype(BF16)
            side_copy(t, d).start()

    order = [(t, d) for t in range(slow) for d in list(range(1, fast)) + [0]]

    def up_copy(a):
        return remote(line_out.at[a], line_in.at[a], u_send.at[a], u_recv.at[a], index(jnp.minimum(s + 1, slow - 1), f, c))

    def down_copy(a):
        slot = jnp.where(a == s - 1, slow, a)
        return remote(line_out.at[a], line_in.at[slot], d_send.at[a], d_recv.at[a], index(jnp.maximum(s - 1, 0), f, c))

    def finish(t):
        a = target(t)
        for d in range(1, fast):
            side_copy(t, d).wait()
        value = kept[0, t]
        for d in range(1, fast):
            value = value + side_in[d, t].astype(F32)
        kept[0, t] = value

        @pl.when(a > s)
        def _():
            @pl.when(s > 0)
            def _():
                up_copy(a).wait_recv()
                line_out[a] = kept[0, t] + line_in[a]

            @pl.when(s == 0)
            def _():
                line_out[a] = kept[0, t]

            up_copy(a).start()

        @pl.when(a < s)
        def _():
            @pl.when(s < slow - 1)
            def _():
                down_copy(a).wait_recv()
                line_out[a] = kept[0, t] + line_in[a]

            @pl.when(s == slow - 1)
            def _():
                line_out[a] = kept[0, t]

            down_copy(a).start()

        @pl.when(a == s)
        def _():
            out[...] = kept[0, t]

    for i, pair in enumerate(order):
        begin(*pair)
        if i:
            middle(*order[i - 1])
    middle(*order[-1])
    for t in range(slow):
        finish(t)

    @pl.when(s > 0)
    def _():
        up_copy(s).wait_recv()
        out[...] += line_in[s]

    @pl.when(s < slow - 1)
    def _():
        down_copy(s).wait_recv()
        out[...] += line_in[slow]

    for a in range(slow):
        pl.when(a > s)(lambda a=a: up_copy(a).wait_send())
        pl.when(a < s)(lambda a=a: down_copy(a).wait_send())


def per_device(n, traces, sketch):
    slow, fast = plan(n)
    parts, rows, sources = traces.shape
    width, share = sketch.shape[1], sketch.shape[2]
    data = traces.reshape(parts * rows, n, share).transpose(1, 0, 2)
    mine = sketch.reshape(parts * width, share)
    dma = pltpu.SemaphoreType.DMA
    vmem = pl.BlockSpec(memory_space=VMEM)
    two = 2 * width
    sketched, gram = pl.pallas_call(
        functools.partial(sketch_kernel, n),
        out_shape=(
            jax.ShapeDtypeStruct((2, rows, width), F32),
            jax.ShapeDtypeStruct((width, width), F32),
        ),
        in_specs=[vmem] * 2,
        out_specs=(vmem, vmem),
        scratch_shapes=[
            VMEM((n, two, share), BF16),
            VMEM((2 * rows, two), F32),
            VMEM((width, width), F32),
            VMEM((width, width), F32),
            VMEM((width, width), F32),
            VMEM((max(fast - 1, 1), width, width), F32),
            VMEM((slow, width, width), F32),
            dma((n,)),
            dma((n,)),
            dma((max(fast - 1, 1), n)),
            dma((n,)),
            dma((n,)),
            dma((slow + fast,)),
            dma((slow + fast,)),
        ],
        compiler_params=pltpu.CompilerParams(
            collective_id=0, has_side_effects=True, vmem_limit_bytes=LIMIT
        ),
        name="gather_sketch",
    )(data, mine)
    scale = math.sqrt(rows * n)
    basis, weights = pl.pallas_call(
        functools.partial(factor_kernel, scale),
        out_shape=(
            jax.ShapeDtypeStruct((2, rows, width), F32),
            jax.ShapeDtypeStruct((two, 2 * rows), BF16),
        ),
        in_specs=[vmem] * 2,
        out_specs=(vmem, vmem),
        compiler_params=pltpu.CompilerParams(vmem_limit_bytes=LIMIT),
        name="factor",
    )(gram, sketched)
    chunk = (two, share)
    coeffs = pl.pallas_call(
        functools.partial(project_kernel, n),
        out_shape=jax.ShapeDtypeStruct(chunk, F32),
        in_specs=[vmem] * 2,
        out_specs=vmem,
        scratch_shapes=[
            VMEM((fast, slow) + chunk, F32),
            VMEM((fast, slow) + chunk, F32),
            VMEM((fast, slow) + chunk, F32),
            VMEM((fast, slow) + chunk, BF16),
            VMEM((fast, slow) + chunk, BF16),
            VMEM((slow,) + chunk, F32),
            VMEM((slow + 1,) + chunk, F32),
            dma((fast, slow)),
            dma((fast, slow)),
            dma((fast, slow)),
            dma((fast, slow)),
            dma((slow,)),
            dma((slow,)),
            dma((slow,)),
            dma((slow,)),
        ],
        compiler_params=pltpu.CompilerParams(
            collective_id=1, has_side_effects=True, vmem_limit_bytes=LIMIT
        ),
        name="project",
    )(data, weights)
    return basis, coeffs.reshape(2, width, share)


def solution(mesh):
    return jax.shard_map(
        functools.partial(per_device, mesh.shape["rcv"]),
        mesh=mesh,
        in_specs=(P(None, ("grp", "rcv"), None), P(None, None, "rcv")),
        out_specs=(P(None, ("grp", "rcv"), None), P(None, "grp", "rcv")),
        check_vma=False,
    )
```

time: 339 us -> 91.1 us (0.27)
  waiting for transfers between devices: 214 us -> 0 us
  Pallas kernels: 0 us -> 81.7 us
  other arithmetic: 53.5 us -> 0 us
  local copies, waits for them, and re-layouts: 44.2 us -> 8.46 us
  between operations: 15.3 us -> 0.65 us
  matrix products: 10.8 us -> 0 us
    psum x1 -> x0, waiting for transfers between devices: 87.7 us -> none  [per_device(): total_re, total_im = lax.psum((gram_re, gram_im), 'rcv')]
    pallas_call x0 -> x3, Pallas kernels: none -> 81.7 us  [the longest x1 36.5 us: per_device(): pl.pallas_call(functools.partial(sketch_kernel, n), out_shape=(jax.ShapeD...]
    unnamed x4 -> x0, waiting for transfers between devices: 78.4 us -> none
    another operation x20 -> x0, other arithmetic: 51.1 us -> none  [the longest x7 28.7 us: factor(): lower = jnp.linalg.cholesky(embed)]
    all_gather x1 -> x0, waiting for transfers between devices: 47.9 us -> none  [per_device(): piece = lax.all_gather(sketch, 'rcv', axis=2, tiled=True)]
    unnamed x11 -> x1, local copies, waits for them, and re-layouts: 20.6 us -> 1.7 us
    slice x3 -> x0, local copies, waits for them, and re-layouts: 10.6 us -> none  [the longest x1 8.06 us: per_device(): piece[1]]
    dot_general x16 -> x0, matrix products: 9.53 us -> none  [the longest x4 4.65 us: across_sources(): lax.dot_general(left, right, (((1,), (1,)), ((), ())), preferred_element_...]
  transfers between devices with their start and end apart: 3 -> 0, of which waited for: 3 -> 0; matrix products, arithmetic and copies ran while one was open for 0% -> 0% of each run, Pallas kernels for 0% -> 0%
where the time goes in v1:
time: 91.1 us; the launch traced here: 90.8 us
  Pallas kernels  81.7 us (90%)
  local copies, waits for them, and re-layouts  8.46 us (9%)
    pallas_call x1, Pallas kernels, per_device(): pl.pallas_call(functools.partial(sketch_kernel, n), out_shape=(jax.ShapeD...  36.5 us
    pallas_call x1, Pallas kernels, per_device(): pl.pallas_call(functools.partial(project_kernel, n), out_shape=jax.ShapeD...  34.7 us
    pallas_call x1, Pallas kernels, per_device(): pl.pallas_call(functools.partial(factor_kernel, scale), out_shape=(jax.Sh...  10.5 us
    reshape x2, local copies, waits for them, and re-layouts, per_device(): data = traces.reshape(parts * rows, n, share).transpose(1, 0, 2)  6.76 us

profile of v1, /device:TPU:0, one launch (start us, length us, event | category | flops | bytes accessed | tf_op | source)
XLA Modules:
  0.0 90.8 jit_solution(11865175999097395316)
XLA Ops:
  0.6 4.8 %reshape.13 = bf16[192,16,336]{2,1,0:T(8,128)(2,1)S(1)} reshape(bf16[2,96,5376]{2,1,0:T(8,128)(2,1)} %param.2) | data formatting | bytes 4128768 | tf_op jit(solution)/shard_map/reshape | solution.py:392
  5.4 2.0 %copy.6 = bf16[192,16,336]{2,0,1:T(8,128)(2,1)} copy(bf16[192,16,336]{2,1,0:T(8,128)(2,1)S(1)} %reshape.13) | data formatting | bytes 4128768 | tf_op jit(solution)/shard_map/reshape | solution.py:392
  7.4 36.5 %gather_sketch.1 = (f32[2,96,96]{2,1,0:T(8,128)}, f32[96,96]{1,0:T(8,128)}) custom-call(bf16[16,192,336]{2,1,0:T(8,128)(2,1)} %bitcast.5, bf16[192,336]{1,0:T(8,128)(2,1)} %bitcast.8), custom_call_target="tpu_custom_call" | custom-call | tf_op jit(solution)/shard_map/gather_sketch/pallas_call | solution.py:397
  43.9 10.5 %factor.1 = (f32[2,96,96]{2,1,0:T(8,128)}, bf16[192,192]{1,0:T(8,128)(2,1)}) custom-call(f32[96,96]{1,0:T(8,128)} %get-tuple-element.6.gram, f32[2,96,96]{2,1,0:T(8,128)} %get-tuple-element.7.sketched), custom_call_target="tpu_custom_call" | custom-call | tf_op jit(solution)/shard_map/factor/pallas_call | solution.py:427
  54.4 34.7 %project.1 = f32[192,336]{1,0:T(8,128)} custom-call(bf16[16,192,336]{2,1,0:T(8,128)(2,1)} %bitcast.6, bf16[192,192]{1,0:T(8,128)(2,1)} %get-tuple-element.9.weights), custom_call_target="tpu_custom_call" | custom-call | tf_op jit(solution)/shard_map/project/pallas_call | solution.py:439
  89.1 1.7 %copy.8 = f32[2,96,336]{2,1,0:T(8,128)} copy(f32[2,96,336]{2,1,0:T(8,128)} %bitcast.7) | data formatting | bytes 516096

commit v2 on v1

--- a/solution.py
+++ b/solution.py
@@ -270,12 +270,13 @@
 
 
 def project_kernel(
-    n, data, weights, out,
+    n, pieces, data, weights, out,
     kept, away, from_core, side_out, side_in, line_out, line_in,
     c_send, c_recv, s_send, s_recv, u_send, u_recv, d_send, d_recv,
 ):
     slow, fast = plan(n)
     me, s, f, c = place(fast)
+    depth = out.shape[0] // pieces
 
     def index(a, b, e):
         return (a * fast + b) * 2 + e
@@ -285,104 +286,126 @@
     lines = [index((s + d) % slow, f, c) for d in range(1, slow)]
     greet([partner] + sides + lines)
 
+    def rows(p):
+        return pl.ds(p * depth, depth)
+
     def product(slot):
         return jnp.dot(weights[...], data[slot], preferred_element_type=F32)
 
-    def core_copy(t, d):
-        return remote(away.at[d, t], from_core.at[d, t], c_send.at[d, t], c_recv.at[d, t], partner)
-
-    def side_copy(t, d):
-        return remote(side_out.at[d, t], side_in.at[d, t], s_send.at[d, t], s_recv.at[d, t], sides[d - 1])
-
-    low = s < slow - s - 1
+    def core_copy(t, d, p):
+        return remote(away.at[d, t, rows(p)], from_core.at[d, t, rows(p)], c_send.at[d, t, p], c_recv.at[d, t, p], partner)
+
+    def side_copy(t, d, p):
+        return remote(side_out.at[d, t, rows(p)], side_in.at[d, t, rows(p)], s_send.at[d, t, p], s_recv.at[d, t, p], sides[d - 1])
+
+    orders = [
+        sorted(range(slow), key=lambda a: (-abs(a - b), -a if 2 * b < slow else a)) for b in range(slow)
+    ]
 
     def target(t):
-        return jnp.where(low, slow - 1 - t, t)
+        value = 0
+        for b in range(slow):
+            value = value + jnp.where(s == b, orders[b][t], 0)
+        return value
+
+    owners = [target(t) for t in range(slow)]
 
     def begin(t, d):
-        a, b = target(t), (f + d) % fast
+        a, b = owners[t], (f + d) % fast
         away[d, t] = product(index(a, b, 1 - c))
-        core_copy(t, d).start()
+        for p in range(pieces):
+            core_copy(t, d, p).start()
         kept[d, t] = product(index(a, b, c))
 
     def middle(t, d):
-        core_copy(t, d).wait()
-        value = kept[d, t] + from_core[d, t]
-        if d == 0:
-            kept[0, t] = value
-        else:
-            side_out[d, t] = value.astype(BF16)
-            side_copy(t, d).start()
+        for p in range(pieces):
+            core_copy(t, d, p).wait()
+            value = kept[d, t, rows(p)] + from_core[d, t, rows(p)]
+            if d == 0:
+                kept[0, t, rows(p)] = value
+            else:
+                side_out[d, t, rows(p)] = value.astype(BF16)
+                side_copy(t, d, p).start()
 
     order = [(t, d) for t in range(slow) for d in list(range(1, fast)) + [0]]
 
-    def up_copy(a):
-        return remote(line_out.at[a], line_in.at[a], u_send.at[a], u_recv.at[a], index(jnp.minimum(s + 1, slow - 1), f, c))
-
-    def down_copy(a):
+    def up_copy(a, p):
+        return remote(line_out.at[a, rows(p)], line_in.at[a, rows(p)], u_send.at[a, p], u_recv.at[a, p], index(jnp.minimum(s + 1, slow - 1), f, c))
+
+    def down_copy(a, p):
         slot = jnp.where(a == s - 1, slow, a)
-        return remote(line_out.at[a], line_in.at[slot], d_send.at[a], d_recv.at[a], index(jnp.maximum(s - 1, 0), f, c))
+        return remote(line_out.at[a, rows(p)], line_in.at[slot, rows(p)], d_send.at[a, p], d_recv.at[a, p], index(jnp.maximum(s - 1, 0), f, c))
 
     def finish(t):
-        a = target(t)
-        for d in range(1, fast):
-            side_copy(t, d).wait()
-        value = kept[0, t]
-        for d in range(1, fast):
-            value = value + side_in[d, t].astype(F32)
-        kept[0, t] = value
-
-        @pl.when(a > s)
-        def _():
-            @pl.when(s > 0)
+        a = owners[t]
+        for p in range(pieces):
+            for d in range(1, fast):
+                side_copy(t, d, p).wait()
+            value = kept[0, t, rows(p)]
+            for d in range(1, fast):
+                value = value + side_in[d, t, rows(p)].astype(F32)
+
+            if t == slow - 1:
+                out[rows(p)] = value
+                continue
+            kept[0, t, rows(p)] = value
+
+            @pl.when(a > s)
             def _():
-                up_copy(a).wait_recv()
-                line_out[a] = kept[0, t] + line_in[a]
-
-            @pl.when(s == 0)
+                @pl.when(s > 0)
+                def _():
+                    up_copy(a, p).wait_recv()
+                    line_out[a, rows(p)] = kept[0, t, rows(p)] + line_in[a, rows(p)]
+
+                @pl.when(s == 0)
+                def _():
+                    line_out[a, rows(p)] = kept[0, t, rows(p)]
+
+                up_copy(a, p).start()
+
+            @pl.when(a < s)
             def _():
-                line_out[a] = kept[0, t]
-
-            up_copy(a).start()
-
-        @pl.when(a < s)
-        def _():
-            @pl.when(s < slow - 1)
-            def _():
-                down_copy(a).wait_recv()
-                line_out[a] = kept[0, t] + line_in[a]
-
-            @pl.when(s == slow - 1)
-            def _():
-                line_out[a] = kept[0, t]
-
-            down_copy(a).start()
-
-        @pl.when(a == s)
-        def _():
-            out[...] = kept[0, t]
+                @pl.when(s < slow - 1)
+                def _():
+                    down_copy(a, p).wait_recv()
+                    line_out[a, rows(p)] = kept[0, t, rows(p)] + line_in[a, rows(p)]
+
+                @pl.when(s == slow - 1)
+                def _():
+                    line_out[a, rows(p)] = kept[0, t, rows(p)]
+
+                down_copy(a, p).start()
+
+    def settle(i):
+        middle(*order[i])
+        t, d = order[i]
+        if d == 0 and t > 0:
+            finish(t - 1)
 
     for i, pair in enumerate(order):
         begin(*pair)
         if i:
-            middle(*order[i - 1])
-    middle(*order[-1])
-    for t in range(slow):
-        finish(t)
-
-    @pl.when(s > 0)
-    def _():
-        up_copy(s).wait_recv()
-        out[...] += line_in[s]
-
-    @pl.when(s < slow - 1)
-    def _():
-        down_copy(s).wait_recv()
-        out[...] += line_in[slow]
-
-    for a in range(slow):
-        pl.when(a > s)(lambda a=a: up_copy(a).wait_send())
-        pl.when(a < s)(lambda a=a: down_copy(a).wait_send())
+            settle(i - 1)
+    settle(len(order) - 1)
+    finish(slow - 1)
+
+    for p in range(pieces):
+
+        @pl.when(s > 0)
+        def _():
+            up_copy(s, p).wait_recv()
+            out[rows(p)] += line_in[s, rows(p)]
+
+        @pl.when(s < slow - 1)
+        def _():
+            down_copy(s, p).wait_recv()
+            out[rows(p)] += line_in[slow, rows(p)]
+
+    for t in range(slow - 1):
+        a = owners[t]
+        for p in range(pieces):
+            pl.when(a > s)(lambda: up_copy(a, p).wait_send())
+            pl.when(a < s)(lambda: down_copy(a, p).wait_send())
 
 
 def per_device(n, traces, sketch):
@@ -436,8 +459,9 @@
         name="factor",
     )(gram, sketched)
     chunk = (two, share)
+    pieces = 4 if n <= 64 and two % 64 == 0 else 1
     coeffs = pl.pallas_call(
-        functools.partial(project_kernel, n),
+        functools.partial(project_kernel, n, pieces),
         out_shape=jax.ShapeDtypeStruct(chunk, F32),
         in_specs=[vmem] * 2,
         out_specs=vmem,
@@ -449,14 +473,14 @@
             VMEM((fast, slow) + chunk, BF16),
             VMEM((slow,) + chunk, F32),
             VMEM((slow + 1,) + chunk, F32),
-            dma((fast, slow)),
-            dma((fast, slow)),
-            dma((fast, slow)),
-            dma((fast, slow)),
-            dma((slow,)),
-            dma((slow,)),
-            dma((slow,)),
-            dma((slow,)),
+            dma((fast, slow, pieces)),
+            dma((fast, slow, pieces)),
+            dma((fast, slow, pieces)),
+            dma((fast, slow, pieces)),
+            dma((slow, pieces)),
+            dma((slow, pieces)),
+            dma((slow, pieces)),
+            dma((slow, pieces)),
         ],
         compiler_params=pltpu.CompilerParams(
             collective_id=1, has_side_effects=True, vmem_limit_bytes=LIMIT

time: 91.1 us -> 93.7 us (1.029)
  Pallas kernels: 81.7 us -> 84.2 us
    pallas_call x1, Pallas kernels: 34.7 us -> 37.2 us  [per_device(): pl.pallas_call(functools.partial(project_kernel, n, pieces), out_shape=ja...]
where the time goes in v2:
time: 93.7 us; the launch traced here: 93.4 us
  Pallas kernels  84.2 us (90%)
  local copies, waits for them, and re-layouts  8.46 us (9%)
    pallas_call x1, Pallas kernels, per_device(): pl.pallas_call(functools.partial(project_kernel, n, pieces), out_shape=ja...  37.2 us
    pallas_call x1, Pallas kernels, per_device(): pl.pallas_call(functools.partial(sketch_kernel, n), out_shape=(jax.ShapeD...  36.5 us
    pallas_call x1, Pallas kernels, per_device(): pl.pallas_call(functools.partial(factor_kernel, scale), out_shape=(jax.Sh...  10.5 us
    reshape x2, local copies, waits for them, and re-layouts, per_device(): data = traces.reshape(parts * rows, n, share).transpose(1, 0, 2)  6.76 us

profile of v2, /device:TPU:0, one launch (start us, length us, event | category | flops | bytes accessed | tf_op | source)
XLA Modules:
  0.0 93.4 jit_solution(771880423281454488)
XLA Ops:
  0.6 4.8 %reshape.13 = bf16[192,16,336]{2,1,0:T(8,128)(2,1)S(1)} reshape(bf16[2,96,5376]{2,1,0:T(8,128)(2,1)} %param.2) | data formatting | bytes 4128768 | tf_op jit(solution)/shard_map/reshape | solution.py:415
  5.4 2.0 %copy.6 = bf16[192,16,336]{2,0,1:T(8,128)(2,1)} copy(bf16[192,16,336]{2,1,0:T(8,128)(2,1)S(1)} %reshape.13) | data formatting | bytes 4128768 | tf_op jit(solution)/shard_map/reshape | solution.py:415
  7.4 36.5 %gather_sketch.1 = (f32[2,96,96]{2,1,0:T(8,128)}, f32[96,96]{1,0:T(8,128)}) custom-call(bf16[16,192,336]{2,1,0:T(8,128)(2,1)} %bitcast.5, bf16[192,336]{1,0:T(8,128)(2,1)} %bitcast.8), custom_call_target="tpu_custom_call" | custom-call | tf_op jit(solution)/shard_map/gather_sketch/pallas_call | solution.py:420
  43.9 10.5 %factor.1 = (f32[2,96,96]{2,1,0:T(8,128)}, bf16[192,192]{1,0:T(8,128)(2,1)}) custom-call(f32[96,96]{1,0:T(8,128)} %get-tuple-element.6.gram, f32[2,96,96]{2,1,0:T(8,128)} %get-tuple-element.7.sketched), custom_call_target="tpu_custom_call" | custom-call | tf_op jit(solution)/shard_map/factor/pallas_call | solution.py:450
  54.4 37.2 %project.1 = f32[192,336]{1,0:T(8,128)} custom-call(bf16[16,192,336]{2,1,0:T(8,128)(2,1)} %bitcast.6, bf16[192,192]{1,0:T(8,128)(2,1)} %get-tuple-element.9.weights), custom_call_target="tpu_custom_call" | custom-call | tf_op jit(solution)/shard_map/project/pallas_call | solution.py:463
  91.7 1.7 %copy.8 = f32[2,96,336]{2,1,0:T(8,128)} copy(f32[2,96,336]{2,1,0:T(8,128)} %bitcast.7) | data formatting | bytes 516096

commit v3 on v1

v3 whole, which is shorter than its diff:
```python
import functools
import math

import jax
import jax.numpy as jnp
from jax import lax
from jax.experimental import pallas as pl
from jax.experimental.pallas import tpu as pltpu
from jax.sharding import PartitionSpec as P

VMEM = pltpu.VMEM
F32 = jnp.float32
BF16 = jnp.bfloat16
LIMIT = 67_000_000


def plan(n):
    chips = n // 2
    fast = max(d for d in range(1, chips + 1) if chips % d == 0 and d * d <= chips)
    return chips // fast, fast


def exact(left, right, dims):
    return lax.dot_general(
        left, right, (dims, ((), ())), precision=lax.Precision.HIGHEST, preferred_element_type=F32
    )


def remote(src, dst, send, recv, target):
    return pltpu.make_async_remote_copy(
        src_ref=src, dst_ref=dst, send_sem=send, recv_sem=recv,
        device_id={"rcv": target}, device_id_type=pl.DeviceIdType.MESH,
    )


def place(fast):
    me = lax.axis_index("rcv")
    chip = me // 2
    return me, chip // fast, chip % fast, me % 2


def greet(targets):
    barrier = pltpu.get_barrier_semaphore()
    for target in targets:
        pl.semaphore_signal(
            barrier, inc=1, device_id={"rcv": target}, device_id_type=pl.DeviceIdType.MESH
        )
    pl.semaphore_wait(barrier, len(targets))


def factor(scale, gram, sketched, basis, weights):
    packed = gram[...]
    width = packed.shape[0]
    turned = packed.T
    row = lax.broadcasted_iota(jnp.int32, packed.shape, 0)
    col = lax.broadcasted_iota(jnp.int32, packed.shape, 1)
    g_re = jnp.where(col >= row, packed, turned)
    g_im = jnp.where(row > col, packed, jnp.where(row < col, -turned, 0.0))
    tile = 8
    count = width // tile
    re = [g_re[tile * i : tile * (i + 1)] for i in range(count)]
    im = [g_im[tile * i : tile * (i + 1)] for i in range(count)]
    lane = lax.broadcasted_iota(jnp.int32, (tile, width), 1)
    sub = lax.broadcasted_iota(jnp.int32, (tile, width), 0)
    for k in range(width):
        at, inside = divmod(k, tile)
        d = re[at][inside : inside + 1, k : k + 1]
        here = lane[:1] == k
        p_re = jnp.where(here, 1.0, re[at][inside : inside + 1, :])
        p_im = jnp.where(here, 0.0, im[at][inside : inside + 1, :])
        inv = 1.0 / d
        q_re = p_re * inv
        q_im = p_im * inv
        for i in range(at, count):
            c_re = re[i][:, k : k + 1]
            c_im = im[i][:, k : k + 1]
            old_re = jnp.where(lane == k, 0.0, re[i])
            old_im = jnp.where(lane == k, 0.0, im[i])
            new_re = old_re - (c_re * q_re - c_im * q_im)
            new_im = old_im - (c_re * q_im + c_im * q_re)
            if i == at:
                root = lax.rsqrt(d)
                new_re = jnp.where(sub > inside, new_re, jnp.where(sub == inside, jnp.where(lane > k, 0.0, p_re * root), re[i]))
                new_im = jnp.where(sub > inside, new_im, jnp.where(sub == inside, jnp.where(lane > k, 0.0, p_im * root), im[i]))
            re[i] = new_re
            im[i] = new_im
    l_re = jnp.concatenate(re, axis=0)
    l_im = jnp.concatenate(im, axis=0)
    s_re, s_im = sketched[0], sketched[1]
    last = ((1,), (1,))
    o_re = exact(s_re, l_re, last) + exact(s_im, l_im, last)
    o_im = exact(s_im, l_re, last) - exact(s_re, l_im, last)
    basis[0] = o_re * scale
    basis[1] = o_im * scale
    t_re, t_im = o_re.T, o_im.T
    rows = o_re.shape[0]
    weights[:width, :rows] = t_re.astype(BF16)
    weights[:width, rows:] = t_im.astype(BF16)
    weights[width:, :rows] = (-t_im).astype(BF16)
    weights[width:, rows:] = t_re.astype(BF16)


def project(
    n, pieces, data, weights, out, held,
    kept, fresh, away, from_core, line_out, line_in,
    c_send, c_recv, s_send, s_recv, u_send, u_recv, d_send, d_recv,
):
    slow, fast = plan(n)
    me, s, f, c = place(fast)
    depth = out.shape[0] // pieces

    def index(a, b, e):
        return (a * fast + b) * 2 + e

    partner = index(s, f, 1 - c)
    sides = [index(s, (f + d) % fast, c) for d in range(1, fast)]

    def rows(p):
        return pl.ds(p * depth, depth)

    def product(slot):
        return jnp.dot(weights[...], data[slot], preferred_element_type=F32)

    def core_copy(t, d, p):
        return remote(away.at[d, t, rows(p)], from_core.at[d, t, rows(p)], c_send.at[d, t, p], c_recv.at[d, t, p], partner)

    def side_copy(t, d, p):
        return remote(held.at[d * slow + t, rows(p)], held.at[n // 2 + d * slow + t, rows(p)], s_send.at[d, t, p], s_recv.at[d, t, p], sides[d - 1])

    orders = [
        sorted(range(slow), key=lambda a: (-abs(a - b), -a if 2 * b < slow else a)) for b in range(slow)
    ]

    def target(t):
        value = 0
        for b in range(slow):
            value = value + jnp.where(s == b, orders[b][t], 0)
        return value

    owners = [target(t) for t in range(slow)]

    def begin(t, d):
        a, b = owners[t], (f + d) % fast
        away[d, t] = product(index(a, b, 1 - c))
        for p in range(pieces):
            core_copy(t, d, p).start()

    def middle(t, d):
        into = kept.at[t] if d == 0 else fresh
        into[...] = product(index(owners[t], (f + d) % fast, c))
        for p in range(pieces):
            core_copy(t, d, p).wait()
            value = into[rows(p)] + from_core[d, t, rows(p)]
            if d == 0:
                kept[t, rows(p)] = value
            else:
                held[d * slow + t, rows(p)] = value.astype(BF16)
                side_copy(t, d, p).start()

    order = [(t, d) for t in range(slow) for d in list(range(1, fast)) + [0]]

    def up_copy(a, p):
        return remote(line_out.at[a, rows(p)], line_in.at[a, rows(p)], u_send.at[a, p], u_recv.at[a, p], index(jnp.minimum(s + 1, slow - 1), f, c))

    def down_copy(a, p):
        slot = jnp.where(a == s - 1, slow, a)
        return remote(line_out.at[a, rows(p)], line_in.at[slot, rows(p)], d_send.at[a, p], d_recv.at[a, p], index(jnp.maximum(s - 1, 0), f, c))

    def finish(t):
        a = owners[t]
        for p in range(pieces):
            for d in range(1, fast):
                side_copy(t, d, p).wait()
            value = kept[t, rows(p)]
            for d in range(1, fast):
                value = value + held[n // 2 + d * slow + t, rows(p)].astype(F32)

            if t == slow - 1:
                out[rows(p)] = value
                continue
            kept[t, rows(p)] = value

            @pl.when(a > s)
            def _():
                @pl.when(s > 0)
                def _():
                    up_copy(a, p).wait_recv()
                    line_out[a, rows(p)] = kept[t, rows(p)] + line_in[a, rows(p)]

                @pl.when(s == 0)
                def _():
                    line_out[a, rows(p)] = kept[t, rows(p)]

                up_copy(a, p).start()

            @pl.when(a < s)
            def _():
                @pl.when(s < slow - 1)
                def _():
                    down_copy(a, p).wait_recv()
                    line_out[a, rows(p)] = kept[t, rows(p)] + line_in[a, rows(p)]

                @pl.when(s == slow - 1)
                def _():
                    line_out[a, rows(p)] = kept[t, rows(p)]

                down_copy(a, p).start()

    def settle(i):
        middle(*order[i])
        t, d = order[i]
        if d == 0 and t > 0:
            finish(t - 1)

    for i, pair in enumerate(order):
        begin(*pair)
        if i:
            settle(i - 1)
    settle(len(order) - 1)
    finish(slow - 1)

    for p in range(pieces):

        @pl.when(s > 0)
        def _():
            up_copy(s, p).wait_recv()
            out[rows(p)] += line_in[s, rows(p)]

        @pl.when(s < slow - 1)
        def _():
            down_copy(s, p).wait_recv()
            out[rows(p)] += line_in[slow, rows(p)]

    for t in range(slow - 1):
        a = owners[t]
        for p in range(pieces):
            pl.when(a > s)(lambda: up_copy(a, p).wait_send())
            pl.when(a < s)(lambda: down_copy(a, p).wait_send())


def kernel(
    n, pieces, scale, traces, mine, basis, out,
    data, sketched, gram, weights,
    held, acc, own, pair_in, pair_sum, quick_in, line_in,
    up_send, down_send, side_send, core_send, recv,
    g_send, g_recv, *project_scratch,
):
    slow, fast = plan(n)
    me, s, f, c = place(fast)
    half = sketched.shape[1]

    def index(a, b, e):
        return (a * fast + b) * 2 + e

    partner = index(s, f, 1 - c)
    sides = [index(s, (f + d) % fast, c) for d in range(1, fast)]
    lines = [index((s + d) % slow, f, c) for d in range(1, slow)]
    greet([partner] + sides + lines)

    def block(slot, first):
        return mine if first else held.at[slot]

    def to_up(slot, first=False):
        return remote(block(slot, first), held.at[slot], up_send.at[slot], recv.at[slot], index(jnp.minimum(s + 1, slow - 1), f, c))

    def to_down(slot, first=False):
        return remote(block(slot, first), held.at[slot], down_send.at[slot], recv.at[slot], index(jnp.maximum(s - 1, 0), f, c))

    def to_side(d, slot, first=False):
        return remote(block(slot, first), held.at[slot], side_send.at[d, slot], recv.at[slot], sides[d])

    def to_core(slot, first=False):
        return remote(block(slot, first), held.at[slot], core_send.at[slot], recv.at[slot], partner)

    def arrived(slot):
        remote(held.at[slot], held.at[slot], core_send.at[slot], recv.at[slot], partner).wait_recv()

    def add(slot, first=False):
        value = mine[...] if first else held[slot]
        acc[...] += lax.dot_general(
            data[slot], value, (((1,), (1,)), ((), ())), preferred_element_type=F32
        )

    pl.when(s < slow - 1)(lambda: to_up(me, True).start())
    pl.when(s > 0)(lambda: to_down(me, True).start())
    for d in range(fast - 1):
        to_side(d, me, True).start()
    to_core(me, True).start()
    share = mine.shape[1]
    for j in range(n):
        data[j] = traces[:, j * share : (j + 1) * share]
    acc[...] = jnp.zeros_like(acc)
    add(me, True)

    for d in range(1, slow):

        @pl.when(s - d >= 0)
        def _(d=d):
            slot = index(s - d, f, c)
            arrived(slot)
            pl.when(s < slow - 1)(lambda: to_up(slot).start())
            for e in range(fast - 1):
                to_side(e, slot).start()
            to_core(slot).start()
            add(slot)

        @pl.when(s + d < slow)
        def _(d=d):
            slot = index(s + d, f, c)
            arrived(slot)
            pl.when(s > 0)(lambda: to_down(slot).start())
            for e in range(fast - 1):
                to_side(e, slot).start()
            to_core(slot).start()
            add(slot)

    def across(b):
        for d in range(slow):
            for sign in ((1,) if d == 0 else (-1, 1)):

                @pl.when((s + sign * d >= 0) & (s + sign * d < slow))
                def _(d=d, sign=sign):
                    slot = index(s + sign * d, b, c)
                    arrived(slot)
                    to_core(slot).start()
                    add(slot)

    for d in range(1, fast):
        across((f + d) % fast)

    def other(b):
        for d in range(slow):
            for sign in ((1,) if d == 0 else (-1, 1)):

                @pl.when((s + sign * d >= 0) & (s + sign * d < slow))
                def _(d=d, sign=sign):
                    slot = index(s + sign * d, b, 1 - c)
                    arrived(slot)
                    add(slot)

    for d in range(fast):
        other((f + d) % fast)

    to_core(me, True).wait_send()
    pl.when(s < slow - 1)(lambda: to_up(me, True).wait_send())
    pl.when(s > 0)(lambda: to_down(me, True).wait_send())
    for e in range(fast - 1):
        to_side(e, me, True).wait_send()
    for d in range(1, slow):

        @pl.when(s - d >= 0)
        def _(d=d):
            slot = index(s - d, f, c)
            pl.when(s < slow - 1)(lambda: to_up(slot).wait_send())
            for e in range(fast - 1):
                to_side(e, slot).wait_send()
            to_core(slot).wait_send()

        @pl.when(s + d < slow)
        def _(d=d):
            slot = index(s + d, f, c)
            pl.when(s > 0)(lambda: to_down(slot).wait_send())
            for e in range(fast - 1):
                to_side(e, slot).wait_send()
            to_core(slot).wait_send()

    for d in range(1, fast):
        for a in range(slow):
            to_core(index(a, (f + d) % fast, c)).wait_send()

    rows = half
    width = sketched.shape[2]
    re = acc[:rows, :width] - acc[rows:, width:]
    im = acc[:rows, width:] + acc[rows:, :width]
    sketched[0] = re
    sketched[1] = im
    first = ((0,), (0,))
    gram_re = exact(re, re, first) + exact(im, im, first)
    gram_im = exact(re, im, first) - exact(im, re, first)
    row = lax.broadcasted_iota(jnp.int32, gram_re.shape, 0)
    col = lax.broadcasted_iota(jnp.int32, gram_re.shape, 1)
    own[...] = jnp.where(col >= row, gram_re, gram_im)

    step = remote(own, pair_in, g_send.at[0], g_recv.at[0], partner)
    step.start()
    step.wait()
    pair_sum[...] = own[...] + pair_in[...]
    steps = [
        remote(pair_sum, quick_in.at[d], g_send.at[1 + d], g_recv.at[1 + d], sides[d])
        for d in range(fast - 1)
    ]
    for step in steps:
        step.start()
    for step in steps:
        step.wait()
    total = pair_sum[...]
    for d in range(fast - 1):
        total = total + quick_in[d]
    line_in[s] = total
    steps = [
        remote(line_in.at[s], line_in.at[s], g_send.at[fast + d], g_recv.at[fast + d], lines[d])
        for d in range(slow - 1)
    ]
    for step in steps:
        step.start()
    for d in range(slow - 1):
        steps[d].wait()
    total = line_in[0]
    for a in range(1, slow):
        total = total + line_in[a]
    gram[...] = total
    factor(scale, gram, sketched, basis, weights)
    project(n, pieces, data, weights, out, held, *project_scratch)


def per_device(n, traces, sketch):
    slow, fast = plan(n)
    parts, rows, sources = traces.shape
    width, share = sketch.shape[1], sketch.shape[2]
    dma = pltpu.SemaphoreType.DMA
    vmem = pl.BlockSpec(memory_space=VMEM)
    two = 2 * width
    chunk = (two, share)
    pieces = 4 if n <= 64 and two % 64 == 0 else 1
    scale = math.sqrt(rows * n)
    square = (width, width)
    basis, coeffs = pl.pallas_call(
        functools.partial(kernel, n, pieces, scale),
        out_shape=(
            jax.ShapeDtypeStruct((2, rows, width), F32),
            jax.ShapeDtypeStruct(chunk, F32),
        ),
        in_specs=[vmem] * 2,
        out_specs=(vmem, vmem),
        scratch_shapes=[
            VMEM((n, 2 * rows, share), BF16),
            VMEM((2, rows, width), F32),
            VMEM(square, F32),
            VMEM((two, 2 * rows), BF16),
            VMEM((n, two, share), BF16),
            VMEM((2 * rows, two), F32),
            VMEM(square, F32),
            VMEM(square, F32),
            VMEM(square, F32),
            VMEM((max(fast - 1, 1),) + square, F32),
            VMEM((slow,) + square, F32),
            dma((n,)),
            dma((n,)),
            dma((max(fast - 1, 1), n)),
            dma((n,)),
            dma((n,)),
            dma((slow + fast,)),
            dma((slow + fast,)),
            VMEM((slow,) + chunk, F32),
            VMEM(chunk, F32),
            VMEM((fast, slow) + chunk, F32),
            VMEM((fast, slow) + chunk, F32),
            VMEM((slow,) + chunk, F32),
            VMEM((slow + 1,) + chunk, F32),
        ]
        + [dma((fast, slow, pieces))] * 4
        + [dma((slow, pieces))] * 4,
        compiler_params=pltpu.CompilerParams(
            collective_id=0, has_side_effects=True, vmem_limit_bytes=LIMIT
        ),
        name="range_finder",
    )(traces.reshape(2 * rows, sources), sketch.reshape(two, share))
    return basis, coeffs.reshape(2, width, share)


def solution(mesh):
    return jax.shard_map(
        functools.partial(per_device, mesh.shape["rcv"]),
        mesh=mesh,
        in_specs=(P(None, ("grp", "rcv"), None), P(None, None, "rcv")),
        out_specs=(P(None, ("grp", "rcv"), None), P(None, "grp", "rcv")),
        check_vma=False,
    )
```

time: 91.1 us -> 81.6 us (0.90)
  local copies, waits for them, and re-layouts: 8.46 us -> 3.23 us
  Pallas kernels: 81.7 us -> 77.5 us
    reshape x2 -> x0, local copies, waits for them, and re-layouts: 6.76 us -> none  [per_device(): data = traces.reshape(parts * rows, n, share).transpose(1, 0, 2)]
    pallas_call x3 -> x1, Pallas kernels: 81.7 us -> 77.5 us  [per_device(): pl.pallas_call(functools.partial(kernel, n, pieces, scale), out_shape=(ja...]
    unnamed x1 -> x2, local copies, waits for them, and re-layouts: 1.7 us -> 3.23 us
where the time goes in v3:
time: 81.6 us; the launch traced here: 81.4 us
  Pallas kernels  77.5 us (95%)
  local copies, waits for them, and re-layouts  3.23 us (4%)
    pallas_call x1, Pallas kernels, per_device(): pl.pallas_call(functools.partial(kernel, n, pieces, scale), out_shape=(ja...  77.5 us
    unnamed x2, local copies, waits for them, and re-layouts  3.23 us

profile of v3, /device:TPU:0, one launch (start us, length us, event | category | flops | bytes accessed | tf_op | source)
XLA Modules:
  0.0 81.4 jit_solution(17186124385572963354)
XLA Ops:
  0.6 77.5 %range_finder.1 = (f32[2,96,96]{2,1,0:T(8,128)}, f32[192,336]{1,0:T(8,128)}) custom-call(bf16[192,5376]{1,0:T(8,128)(2,1)} %bitcast.3, bf16[192,336]{1,0:T(8,128)(2,1)} %bitcast.5), custom_call_target="tpu_custom_call" | custom-call | tf_op jit(solution)/shard_map/range_finder/pallas_call | solution.py:427
  78.1 1.5 %copy.6 = f32[2,96,96]{2,1,0:T(8,128)} copy(f32[2,96,96]{2,1,0:T(8,128)} %get-tuple-element.8) | data formatting | bytes 147456
  79.7 1.7 %copy.7 = f32[2,96,336]{2,1,0:T(8,128)} copy(f32[2,96,336]{2,1,0:T(8,128)} %bitcast.4) | data formatting | bytes 516096

commit v4 on v3

--- a/solution.py
+++ b/solution.py
@@ -102,8 +102,8 @@
 
 def project(
     n, pieces, data, weights, out, held,
-    kept, fresh, away, from_core, line_out, line_in,
-    c_send, c_recv, s_send, s_recv, u_send, u_recv, d_send, d_recv,
+    kept, fresh, away, from_core, line_out, line_in, near_out, near_in,
+    c_send, c_recv, s_send, s_recv, u_send, u_recv, d_send, d_recv, n_send, n_recv,
 ):
     slow, fast = plan(n)
     me, s, f, c = place(fast)
@@ -166,6 +166,16 @@
         slot = jnp.where(a == s - 1, slow, a)
         return remote(line_out.at[a, rows(p)], line_in.at[slot, rows(p)], d_send.at[a, p], d_recv.at[a, p], index(jnp.maximum(s - 1, 0), f, c))
 
+    def near_copy(k, p):
+        goal = index(min(1, slow - 1) if k == 0 else max(slow - 2, 0), f, c)
+        return remote(near_out.at[rows(p)], near_in.at[k, rows(p)], n_send.at[p], n_recv.at[k, p], goal)
+
+    def near_up(a):
+        return (s == 0) & (a == 1)
+
+    def near_down(a):
+        return (s == slow - 1) & (a == slow - 2)
+
     def finish(t):
         a = owners[t]
         for p in range(pieces):
@@ -180,7 +190,17 @@
                 continue
             kept[t, rows(p)] = value
 
-            @pl.when(a > s)
+            @pl.when(near_up(a))
+            def _():
+                near_out[rows(p)] = value.astype(BF16)
+                near_copy(0, p).start()
+
+            @pl.when(near_down(a))
+            def _():
+                near_out[rows(p)] = value.astype(BF16)
+                near_copy(1, p).start()
+
+            @pl.when((a > s) & jnp.logical_not(near_up(a)))
             def _():
                 @pl.when(s > 0)
                 def _():
@@ -193,7 +213,7 @@
 
                 up_copy(a, p).start()
 
-            @pl.when(a < s)
+            @pl.when((a < s) & jnp.logical_not(near_down(a)))
             def _():
                 @pl.when(s < slow - 1)
                 def _():
@@ -221,12 +241,22 @@
 
     for p in range(pieces):
 
-        @pl.when(s > 0)
+        @pl.when(s == 1)
+        def _():
+            near_copy(0, p).wait_recv()
+            out[rows(p)] += near_in[0, rows(p)].astype(F32)
+
+        @pl.when(s == slow - 2)
+        def _():
+            near_copy(1, p).wait_recv()
+            out[rows(p)] += near_in[1, rows(p)].astype(F32)
+
+        @pl.when(s > 1)
         def _():
             up_copy(s, p).wait_recv()
             out[rows(p)] += line_in[s, rows(p)]
 
-        @pl.when(s < slow - 1)
+        @pl.when(s < slow - 2)
         def _():
             down_copy(s, p).wait_recv()
             out[rows(p)] += line_in[slow, rows(p)]
@@ -234,8 +264,10 @@
     for t in range(slow - 1):
         a = owners[t]
         for p in range(pieces):
-            pl.when(a > s)(lambda: up_copy(a, p).wait_send())
-            pl.when(a < s)(lambda: down_copy(a, p).wait_send())
+            pl.when(near_up(a))(lambda: near_copy(0, p).wait_send())
+            pl.when(near_down(a))(lambda: near_copy(1, p).wait_send())
+            pl.when((a > s) & jnp.logical_not(near_up(a)))(lambda: up_copy(a, p).wait_send())
+            pl.when((a < s) & jnp.logical_not(near_down(a)))(lambda: down_copy(a, p).wait_send())
 
 
 def kernel(
@@ -257,23 +289,32 @@
     lines = [index((s + d) % slow, f, c) for d in range(1, slow)]
     greet([partner] + sides + lines)
 
-    def block(slot, first):
-        return mine if first else held.at[slot]
-
-    def to_up(slot, first=False):
-        return remote(block(slot, first), held.at[slot], up_send.at[slot], recv.at[slot], index(jnp.minimum(s + 1, slow - 1), f, c))
-
-    def to_down(slot, first=False):
-        return remote(block(slot, first), held.at[slot], down_send.at[slot], recv.at[slot], index(jnp.maximum(s - 1, 0), f, c))
-
-    def to_side(d, slot, first=False):
-        return remote(block(slot, first), held.at[slot], side_send.at[d, slot], recv.at[slot], sides[d])
-
-    def to_core(slot, first=False):
-        return remote(block(slot, first), held.at[slot], core_send.at[slot], recv.at[slot], partner)
-
-    def arrived(slot):
-        remote(held.at[slot], held.at[slot], core_send.at[slot], recv.at[slot], partner).wait_recv()
+    size = mine.shape[0] // pieces
+
+    def piece(p):
+        return pl.ds(p * size, size)
+
+    def send(kind, slot, p, first, where):
+        source = mine.at[piece(p)] if first else held.at[slot, piece(p)]
+        return remote(source, held.at[slot, piece(p)], kind.at[slot, p], recv.at[slot, p], where)
+
+    above = index(jnp.minimum(s + 1, slow - 1), f, c)
+    below = index(jnp.maximum(s - 1, 0), f, c)
+
+    def to_up(slot, p, first=False):
+        return send(up_send, slot, p, first, above)
+
+    def to_down(slot, p, first=False):
+        return send(down_send, slot, p, first, below)
+
+    def to_side(d, slot, p, first=False):
+        return send(side_send.at[d], slot, p, first, sides[d])
+
+    def to_core(slot, p, first=False):
+        return send(core_send, slot, p, first, partner)
+
+    def arrived(slot, p):
+        to_core(slot, p).wait_recv()
 
     def add(slot, first=False):
         value = mine[...] if first else held[slot]
@@ -281,11 +322,23 @@
             data[slot], value, (((1,), (1,)), ((), ())), preferred_element_type=F32
         )
 
-    pl.when(s < slow - 1)(lambda: to_up(me, True).start())
-    pl.when(s > 0)(lambda: to_down(me, True).start())
-    for d in range(fast - 1):
-        to_side(d, me, True).start()
-    to_core(me, True).start()
+    def spread(act, slot, p, up, down, first=False):
+        if up:
+            pl.when(s < slow - 1)(lambda: act(to_up(slot, p, first)))
+        if down:
+            pl.when(s > 0)(lambda: act(to_down(slot, p, first)))
+        for d in range(fast - 1):
+            act(to_side(d, slot, p, first))
+        act(to_core(slot, p, first))
+
+    def begin(copy):
+        copy.start()
+
+    def sent(copy):
+        copy.wait_send()
+
+    for p in range(pieces):
+        spread(begin, me, p, True, True, True)
     share = mine.shape[1]
     for j in range(n):
         data[j] = traces[:, j * share : (j + 1) * share]
@@ -293,80 +346,47 @@
     add(me, True)
 
     for d in range(1, slow):
-
-        @pl.when(s - d >= 0)
-        def _(d=d):
-            slot = index(s - d, f, c)
-            arrived(slot)
-            pl.when(s < slow - 1)(lambda: to_up(slot).start())
-            for e in range(fast - 1):
-                to_side(e, slot).start()
-            to_core(slot).start()
-            add(slot)
-
-        @pl.when(s + d < slow)
-        def _(d=d):
-            slot = index(s + d, f, c)
-            arrived(slot)
-            pl.when(s > 0)(lambda: to_down(slot).start())
-            for e in range(fast - 1):
-                to_side(e, slot).start()
-            to_core(slot).start()
-            add(slot)
-
-    def across(b):
+        for p in range(pieces):
+
+            @pl.when(s - d >= 0)
+            def _():
+                arrived(index(s - d, f, c), p)
+                spread(begin, index(s - d, f, c), p, True, False)
+
+            @pl.when(s + d < slow)
+            def _():
+                arrived(index(s + d, f, c), p)
+                spread(begin, index(s + d, f, c), p, False, True)
+
+        pl.when(s - d >= 0)(lambda: add(index(s - d, f, c)))
+        pl.when(s + d < slow)(lambda: add(index(s + d, f, c)))
+
+    def remaining(b, e, pass_on):
         for d in range(slow):
-            for sign in ((1,) if d == 0 else (-1, 1)):
+            for sign in (1,) if d == 0 else (-1, 1):
 
                 @pl.when((s + sign * d >= 0) & (s + sign * d < slow))
-                def _(d=d, sign=sign):
-                    slot = index(s + sign * d, b, c)
-                    arrived(slot)
-                    to_core(slot).start()
+                def _():
+                    slot = index(s + sign * d, b, e)
+                    for p in range(pieces):
+                        arrived(slot, p)
+                        if pass_on:
+                            to_core(slot, p).start()
                     add(slot)
 
     for d in range(1, fast):
-        across((f + d) % fast)
-
-    def other(b):
-        for d in range(slow):
-            for sign in ((1,) if d == 0 else (-1, 1)):
-
-                @pl.when((s + sign * d >= 0) & (s + sign * d < slow))
-                def _(d=d, sign=sign):
-                    slot = index(s + sign * d, b, 1 - c)
-                    arrived(slot)
-                    add(slot)
-
+        remaining((f + d) % fast, c, True)
     for d in range(fast):
-        other((f + d) % fast)
-
-    to_core(me, True).wait_send()
-    pl.when(s < slow - 1)(lambda: to_up(me, True).wait_send())
-    pl.when(s > 0)(lambda: to_down(me, True).wait_send())
-    for e in range(fast - 1):
-        to_side(e, me, True).wait_send()
-    for d in range(1, slow):
-
-        @pl.when(s - d >= 0)
-        def _(d=d):
-            slot = index(s - d, f, c)
-            pl.when(s < slow - 1)(lambda: to_up(slot).wait_send())
-            for e in range(fast - 1):
-                to_side(e, slot).wait_send()
-            to_core(slot).wait_send()
-
-        @pl.when(s + d < slow)
-        def _(d=d):
-            slot = index(s + d, f, c)
-            pl.when(s > 0)(lambda: to_down(slot).wait_send())
-            for e in range(fast - 1):
-                to_side(e, slot).wait_send()
-            to_core(slot).wait_send()
-
-    for d in range(1, fast):
-        for a in range(slow):
-            to_core(index(a, (f + d) % fast, c)).wait_send()
+        remaining((f + d) % fast, 1 - c, False)
+
+    for p in range(pieces):
+        spread(sent, me, p, True, True, True)
+        for d in range(1, slow):
+            pl.when(s - d >= 0)(lambda: spread(sent, index(s - d, f, c), p, True, False))
+            pl.when(s + d < slow)(lambda: spread(sent, index(s + d, f, c), p, False, True))
+        for d in range(1, fast):
+            for a in range(slow):
+                to_core(index(a, (f + d) % fast, c), p).wait_send()
 
     rows = half
     width = sketched.shape[2]
@@ -376,7 +396,8 @@
     sketched[1] = im
     first = ((0,), (0,))
     gram_re = exact(re, re, first) + exact(im, im, first)
-    gram_im = exact(re, im, first) - exact(im, re, first)
+    cross = exact(re, im, first)
+    gram_im = cross - cross.T
     row = lax.broadcasted_iota(jnp.int32, gram_re.shape, 0)
     col = lax.broadcasted_iota(jnp.int32, gram_re.shape, 1)
     own[...] = jnp.where(col >= row, gram_re, gram_im)
@@ -444,11 +465,11 @@
             VMEM(square, F32),
             VMEM((max(fast - 1, 1),) + square, F32),
             VMEM((slow,) + square, F32),
-            dma((n,)),
-            dma((n,)),
-            dma((max(fast - 1, 1), n)),
-            dma((n,)),
-            dma((n,)),
+            dma((n, pieces)),
+            dma((n, pieces)),
+            dma((max(fast - 1, 1), n, pieces)),
+            dma((n, pieces)),
+            dma((n, pieces)),
             dma((slow + fast,)),
             dma((slow + fast,)),
             VMEM((slow,) + chunk, F32),
@@ -457,9 +478,12 @@
             VMEM((fast, slow) + chunk, F32),
             VMEM((slow,) + chunk, F32),
             VMEM((slow + 1,) + chunk, F32),
+            VMEM(chunk, BF16),
+            VMEM((2,) + chunk, BF16),
         ]
         + [dma((fast, slow, pieces))] * 4
-        + [dma((slow, pieces))] * 4,
+        + [dma((slow, pieces))] * 4
+        + [dma((pieces,)), dma((2, pieces))],
         compiler_params=pltpu.CompilerParams(
             collective_id=0, has_side_effects=True, vmem_limit_bytes=LIMIT
         ),

time: 81.6 us -> 81.7 us (level)
  no operation moved by 1% of the time
where the time goes in v4:
time: 81.7 us; the launch traced here: 81.4 us
  Pallas kernels  77.6 us (95%)
  local copies, waits for them, and re-layouts  3.23 us (4%)
    pallas_call x1, Pallas kernels, per_device(): pl.pallas_call(functools.partial(kernel, n, pieces, scale), out_shape=(ja...  77.6 us
    unnamed x2, local copies, waits for them, and re-layouts  3.23 us

profile of v4, /device:TPU:0, one launch (start us, length us, event | category | flops | bytes accessed | tf_op | source)
XLA Modules:
  0.0 81.4 jit_solution(15261194475440526980)
XLA Ops:
  0.6 77.6 %range_finder.1 = (f32[2,96,96]{2,1,0:T(8,128)}, f32[192,336]{1,0:T(8,128)}) custom-call(bf16[192,5376]{1,0:T(8,128)(2,1)} %bitcast.3, bf16[192,336]{1,0:T(8,128)(2,1)} %bitcast.5), custom_call_target="tpu_custom_call" | custom-call | tf_op jit(solution)/shard_map/range_finder/pallas_call | solution.py:448
  78.2 1.5 %copy.6 = f32[2,96,96]{2,1,0:T(8,128)} copy(f32[2,96,96]{2,1,0:T(8,128)} %get-tuple-element.8) | data formatting | bytes 147456
  79.7 1.7 %copy.7 = f32[2,96,336]{2,1,0:T(8,128)} copy(f32[2,96,336]{2,1,0:T(8,128)} %bitcast.4) | data formatting | bytes 516096

commit v5 on v4

--- a/solution.py
+++ b/solution.py
@@ -442,7 +442,7 @@
     vmem = pl.BlockSpec(memory_space=VMEM)
     two = 2 * width
     chunk = (two, share)
-    pieces = 4 if n <= 64 and two % 64 == 0 else 1
+    pieces = 2 if n <= 64 and two % 64 == 0 else 1
     scale = math.sqrt(rows * n)
     square = (width, width)
     basis, coeffs = pl.pallas_call(

time: 81.7 us -> 80.3 us (0.983)
  Pallas kernels: 77.6 us -> 76.3 us
    pallas_call x1, Pallas kernels: 77.6 us -> 76.3 us  [per_device(): pl.pallas_call(functools.partial(kernel, n, pieces, scale), out_shape=(ja...]
where the time goes in v5:
time: 80.3 us; the launch traced here: 80.1 us
  Pallas kernels  76.3 us (95%)
  local copies, waits for them, and re-layouts  3.23 us (4%)
    pallas_call x1, Pallas kernels, per_device(): pl.pallas_call(functools.partial(kernel, n, pieces, scale), out_shape=(ja...  76.3 us
    unnamed x2, local copies, waits for them, and re-layouts  3.23 us

profile of v5, /device:TPU:0, one launch (start us, length us, event | category | flops | bytes accessed | tf_op | source)
XLA Modules:
  0.0 80.1 jit_solution(5243396596456610302)
XLA Ops:
  0.6 76.3 %range_finder.1 = (f32[2,96,96]{2,1,0:T(8,128)}, f32[192,336]{1,0:T(8,128)}) custom-call(bf16[192,5376]{1,0:T(8,128)(2,1)} %bitcast.3, bf16[192,336]{1,0:T(8,128)(2,1)} %bitcast.5), custom_call_target="tpu_custom_call" | custom-call | tf_op jit(solution)/shard_map/range_finder/pallas_call | solution.py:448
  76.9 1.5 %copy.6 = f32[2,96,96]{2,1,0:T(8,128)} copy(f32[2,96,96]{2,1,0:T(8,128)} %get-tuple-element.8) | data formatting | bytes 147456
  78.4 1.7 %copy.7 = f32[2,96,336]{2,1,0:T(8,128)} copy(f32[2,96,336]{2,1,0:T(8,128)} %bitcast.4) | data formatting | bytes 516096
